TPU v7x, 32 devices: a whole 2x2x4 slice. The times are simulated.
32 devices in a mesh: row: 8 (over z, y), col: 4 (over x, core).
Axes of the slice: x: 2, y: 2, z: 4, core: 2. Of those that a mesh axis runs over, the one named last changes fastest.
Arguments:
- query_acts: bfloat16 [256, 8192], P('col', 'row'), may hold values from -6 to 6
- query_grads: bfloat16 [256, 28672], P('row', 'col'), may hold values from -6 to 6
- ritz_mats: float32 [3, 8192, 28672], P(None, 'row', 'col'), may hold values from -0.095683193 to 0.095683193, as said below
- eigenvalues: float32 [3], replicated, may hold values from 0.5 to 4
- train_acts: bfloat16 [64, 8192], P('row'), may hold values from -6 to 6
- train_grads: bfloat16 [64, 28672], P('row', 'col'), may hold values from -6 to 6
Outputs:
- response: bfloat16 [64, 28672], P('row', 'col')
- scores: float32 [64], P('row')
Inputs may be any that keep to these rules, and one draw needn't show every extreme that they name: `ritz_mats`: real entries of order one over the square root of 8192; every matrix has full rank.
All inputs are finite; a program needn't handle non-finite values.
Results may differ from a plain program's by a relative error of at most 0.0012.
Values may be sent and summed in bfloat16 or wider, within the bound.
No kernel may reach another device: no remote copies, remote signals or barrier semaphores. Data moves between devices by JAX's collectives and lax.ppermute only.
A program may use at most 192 MiB of HBM per device.

v0:
```python
import math
import jax
import jax.numpy as jnp
from jax import lax
from jax.sharding import PartitionSpec as P

D_OUT = 28672
QUERY = 256
highest = lax.Precision.HIGHEST


def per_device(query_acts, query_grads, ritz_mats, eigenvalues, train_acts, train_grads):
    outer_cols = ritz_mats.shape[2]
    acts_all = lax.all_gather(query_acts, "col", axis=0, tiled=True)
    grad_tile = lax.dot_general(
        acts_all,
        lax.all_gather(query_grads, "row", axis=0, tiled=True),
        (((0,), (0,)), ((), ())),
        preferred_element_type=jnp.float32,
    )
    local_terms = jnp.sum(ritz_mats * grad_tile[None], axis=(1, 2))
    coeffs = lax.psum(local_terms, ("row", "col"))
    weights = coeffs / (eigenvalues * math.sqrt(QUERY * D_OUT))
    train_local = lax.all_to_all(train_acts, "row", split_axis=1, concat_axis=0, tiled=True).astype(
        jnp.float32
    )
    root_width = math.sqrt(D_OUT)
    total = jnp.zeros((lax.axis_size("row") * train_acts.shape[0], outer_cols), jnp.float32)
    for which in range(ritz_mats.shape[0]):
        total = total + weights[which] * jnp.dot(train_local, ritz_mats[which], precision=highest)
    response_full = lax.psum_scatter(total, "row", scatter_dimension=0, tiled=True)
    score_terms = jnp.sum(response_full * train_grads.astype(jnp.float32), axis=1) / root_width
    scores = lax.psum(score_terms, "col")
    response = response_full.astype(jnp.bfloat16)
    return (response, scores)


def solution(mesh):
    in_specs = (
        P("col", "row"),
        P("row", "col"),
        P(None, "row", "col"),
        P(),
        P("row", None),
        P("row", "col"),
    )
    out_specs = (P("row", "col"), P("row"))
    return jax.shard_map(
        per_device, mesh=mesh, in_specs=in_specs, out_specs=out_specs, check_vma=False
    )
```

profile of v0, /device:TPU:0, one launch (start us, length us, event | category | flops | bytes accessed | tf_op | source)
XLA Modules:
  0.0 306.3 jit_solution(11983988093099938950)
XLA Ops:
  7.2 0.0 all-gather.2.cloned.1.call-start
  7.2 0.7 all-gather.2.cloned.1.call-update
  7.9 8.9 %all_gather.6 = bf16[256,1024]{1,0:T(8,128)(2,1)S(1)} all-gather(bf16[64,1024]{1,0:T(8,128)(2,1)} %param.6), channel_id=1, replica_groups=mesh['row'=8,'col'=4] {'col'}, dimensions={0}, use_global_device_ids=true | all-gather | bytes 655360 | tf_op jit(solution)/shard_map/all_gather | solution.py:14
  16.8 62.4 %all-gather.2.cloned.1.call-done = bf16[256,7168]{1,0:T(8,128)(2,1)} async-done(((bf16[32,7168]{1,0:T(8,128)(2,1)}), bf16[256,7168]{1,0:T(8,128)(2,1)}) %all-gather.2.cloned.1.call-update) | async-done | bytes 3670032 | tf_op jit(solution)/shard_map/all_gather | solution.py:17
  79.1 13.7 %fusion.28 = f32[1024,7168]{1,0:T(8,128)} fusion(bf16[256,1024]{1,0:T(8,128)(2,1)S(1)} %all_gather.6, bf16[256,7168]{1,0:T(8,128)(2,1)} %all-gather.2.cloned.1.call-done), kind=kOutput, calls=%fused_computation.22 | convolution fusion | flops 3758096384 | bytes 33554432 | tf_op jit(solution)/shard_map/dot_general | solution.py:15
  92.8 0.0 copy-start.1
  92.8 35.5 %multiply_reduce_fusion = f32[3]{0:T(128)S(1)} fusion(f32[3,1024,7168]{2,1,0:T(8,128)} %param.8, f32[1024,7168]{1,0:T(8,128)} %fusion.28), kind=kLoop, calls=%fused_computation | loop fusion | flops 44040188 | bytes 117440528 | tf_op jit(solution)/shard_map/reduce_sum | solution.py:21
  128.4 3.4 %all-to-all-start = ((bf16[8,8,1024]{2,0,1:T(8,128)(2,1)}), bf16[8,8,1024]{2,0,1:T(8,128)(2,1)S(1)}, u32[]{:S(2)}, u32[]{:S(2)}) async-start(bf16[8,8,1024]{2,0,1:T(8,128)(2,1)} %bitcast.1), calls=%async_computation | async-start | bytes 262144 | tf_op jit(solution)/shard_map/all_to_all | solution.py:24
  131.8 0.0 reduce-scatter.2.cloned.1.call-start
  131.8 40.7 %psum.14 = f32[3]{0:T(128)S(1)} all-reduce(f32[3]{0:T(128)S(1)} %multiply_reduce_fusion), channel_id=1, replica_groups=mesh['row'=8,'col'=4] {'row','col'}, use_global_device_ids=true, to_apply=%region_1.0 | all-reduce | flops 3 | bytes 24 | tf_op jit(solution)/shard_map/psum | solution.py:22
  172.5 0.0 copy-done.1
  172.5 0.7 fusion.27
  173.2 0.0 all-to-all-done
  173.2 15.6 %fusion.15 = f32[64,7168]{1,0:T(8,128)S(1)} fusion(f32[3,1024,7168]{2,1,0:T(8,128)} %param.8, f32[]{:T(128)} %bitcast.5, bf16[8,8,1024]{2,0,1:T(8,128)(2,1)S(1)} %all-to-all-done), kind=kOutput, calls=%fused_computation.12 | convolution fusion | flops 5637603328 | bytes 31326720 | tf_op jit(solution)/shard_map/dot_general | solution.py:30
  188.8 18.0 %fusion.12 = f32[64,7168]{1,0:T(8,128)S(1)} fusion(f32[64,7168]{1,0:T(8,128)S(1)} %fusion.15, f32[3,1024,7168]{2,1,0:T(8,128)} %param.8, f32[]{:T(128)} %bitcast, bf16[8,8,1024]{2,0,1:T(8,128)(2,1)S(1)} %all-to-all-done), kind=kOutput, calls=%fused_computation.11 | convolution fusion | flops 5638062080 | bytes 33161728 | tf_op jit(solution)/shard_map/dot_general | solution.py:30
  206.8 0.0 copy-start
  206.8 17.5 %fusion.21 = f32[64,7168]{1,0:T(8,128)} fusion(f32[64,7168]{1,0:T(8,128)S(1)} %fusion.12, f32[3,1024,7168]{2,1,0:T(8,128)} %param.8, f32[]{:T(128)} %bitcast.8, bf16[8,8,1024]{2,0,1:T(8,128)(2,1)S(1)} %all-to-all-done), kind=kOutput, calls=%fused_computation.14 | convolution fusion | flops 5638062080 | bytes 33161728 | tf_op jit(solution)/shard_map/dot_general | solution.py:30
  224.3 0.0 reduce-scatter.2.cloned.1.call-update
  224.3 67.2 %reduce-scatter.2.cloned.1.call-done = f32[8,7168]{1,0:T(8,128)} async-done(((f32[64,7168]{1,0:T(8,128)}), f32[8,7168]{1,0:T(8,128)}) %reduce-scatter.2.cloned.1.call-update) | async-done | bytes 229392 | tf_op jit(solution)/shard_map/reduce_scatter | solution.py:31
  291.5 0.0 copy-done
  291.5 1.8 multiply_reduce_fusion.1
  293.3 6.2 %psum.15 = f32[8]{0:T(128)} all-reduce(f32[8]{0:T(128)S(1)} %broadcast_multiply_fusion), channel_id=1, replica_groups=mesh['row'=8,'col'=4] {'col'}, use_global_device_ids=true, to_apply=%region_4.0 | all-reduce | flops 8 | bytes 64 | tf_op jit(solution)/shard_map/psum | solution.py:33
  (2 shorter events, 0.0 us)
Async XLA Ops:
  7.2 72.0 %all-gather.2.cloned.1.call-start = ((), (), s32[]{:S(2)}) async-start(), calls=%async_computation.2 | async-start | bytes 4128768 | tf_op jit(solution)/shard_map/all_gather | solution.py:17
  92.8 79.7 %copy-start.1 = (f32[3]{0:T(128)S(1)}, f32[3]{0:T(128)}, u32[]{:S(2)}) copy-start(f32[3]{0:T(128)} %param.9) | copy-start | bytes 40
  128.4 44.8 %all-to-all-start = ((bf16[8,8,1024]{2,0,1:T(8,128)(2,1)}), bf16[8,8,1024]{2,0,1:T(8,128)(2,1)S(1)}, u32[]{:S(2)}, u32[]{:S(2)}) async-start(bf16[8,8,1024]{2,0,1:T(8,128)(2,1)} %bitcast.1), calls=%async_computation | async-start | bytes 262144 | tf_op jit(solution)/shard_map/all_to_all | solution.py:24
  131.8 159.8 %reduce-scatter.2.cloned.1.call-start = ((), (), s32[]{:S(2)}) async-start(), calls=%async_computation.3 | async-start | bytes 2064384 | tf_op jit(solution)/shard_map/reduce_scatter | solution.py:31
  206.8 84.7 %copy-start = (bf16[8,7168]{1,0:T(8,128)(2,1)S(1)}, bf16[8,7168]{1,0:T(8,128)(2,1)}, u32[]{:S(2)}) copy-start(bf16[8,7168]{1,0:T(8,128)(2,1)} %param.11) | copy-start | bytes 344068
Sparse Core Ops, SparseCore 0:
  10.2 68.9 all-gather.1
  224.4 67.0 reduce-scatter.1
where the time goes:
time: 307 us; the launch traced here: 306 us
  waiting for transfers between devices  130 us (42%)
  matrix products  64.8 us (21%)
  blocking collectives  55.7 us (18%)
  other arithmetic  37.4 us (12%)
  between operations  14.1 us (5%)
  starting transfers between devices  3.46 us (1%)
    reduce_scatter x1, waiting for transfers between devices, per_device(): lax.psum_scatter(total, 'row', scatter_dimension=0, tiled=True)  67.2 us
    all_gather x1, waiting for transfers between devices, per_device(): lax.all_gather(query_grads, 'row', axis=0, tiled=True)  62.4 us
    dot_general x3, matrix products, per_device(): jnp.dot(train_local, ritz_mats[which], precision=highest)  51.1 us
    psum x1, blocking collectives, per_device(): coeffs = lax.psum(local_terms, ('row', 'col'))  40.7 us
    reduce_sum x1, other arithmetic, per_device(): local_terms = jnp.sum(ritz_mats * grad_tile[None], axis=(1, 2))  35.5 us
    dot_general x1, matrix products, per_device(): lax.dot_general(acts_all, lax.all_gather(query_grads, 'row', axis=0, tile...  13.7 us
    all_gather x1, blocking collectives, per_device(): acts_all = lax.all_gather(query_acts, 'col', axis=0, tiled=True)  8.86 us
    psum x1, blocking collectives, per_device(): scores = lax.psum(score_terms, 'col')  6.17 us
  transfers between devices with their start and end apart: 3, of which 2 were waited for; matrix products, arithmetic and copies ran while one was open for 0% of the time, Pallas kernels for 0%

commit v1 on v0

--- a/solution.py
+++ b/solution.py
@@ -1,3 +1,4 @@
+import functools
 import math
 import jax
 import jax.numpy as jnp
@@ -7,6 +8,14 @@
 D_OUT = 28672
 QUERY = 256
 highest = lax.Precision.HIGHEST
+
+
+def shards_supply(t0, comm_axis):
+    x_new = jax.lax.all_gather(t0, axis_name=comm_axis)
+    return jnp.sum(x_new, axis=0)
+
+
+plan_row = functools.partial(shards_supply, comm_axis=("row", "col"))
 
 
 def per_device(query_acts, query_grads, ritz_mats, eigenvalues, train_acts, train_grads):
@@ -19,7 +28,7 @@
         preferred_element_type=jnp.float32,
     )
     local_terms = jnp.sum(ritz_mats * grad_tile[None], axis=(1, 2))
-    coeffs = lax.psum(local_terms, ("row", "col"))
+    coeffs = plan_row(local_terms)
     weights = coeffs / (eigenvalues * math.sqrt(QUERY * D_OUT))
     train_local = lax.all_to_all(train_acts, "row", split_axis=1, concat_axis=0, tiled=True).astype(
         jnp.float32

time: 307 us -> 303 us (0.987)
  waiting for transfers between devices: 130 us -> 125 us
  starting transfers between devices: 3.46 us -> 7.4 us
    psum x1 -> x0, blocking collectives: 40.7 us -> none  [per_device(): coeffs = lax.psum(local_terms, ('row', 'col'))]
    unnamed x0 -> x1, blocking collectives: none -> 39.3 us
    all_gather x1, waiting for transfers between devices: 62.4 us -> 56.5 us  [per_device(): lax.all_gather(query_grads, 'row', axis=0, tiled=True)]
    all_to_all x1, starting transfers between devices: 3.38 us -> 7.32 us  [per_device(): lax.all_to_all(train_acts, 'row', split_axis=1, concat_axis=0, tiled=True)]
  transfers between devices with their start and end apart: 3 -> 3, of which waited for: 2 -> 2; matrix products, arithmetic and copies ran while one was open for 0% -> 17% of each run, Pallas kernels for 0% -> 0%
where the time goes in v1:
time: 303 us; the launch traced here: 302 us
  waiting for transfers between devices  125 us (41%)
  matrix products  64.8 us (21%)
  blocking collectives  52.8 us (17%)
  other arithmetic  37.4 us (12%)
  between operations  14.1 us (5%)
  starting transfers between devices  7.4 us (2%)
    reduce_scatter x1, waiting for transfers between devices, per_device(): lax.psum_scatter(total, 'row', scatter_dimension=0, tiled=True)  67.6 us
    all_gather x1, waiting for transfers between devices, per_device(): lax.all_gather(query_grads, 'row', axis=0, tiled=True)  56.5 us
    dot_general x3, matrix products, per_device(): jnp.dot(train_local, ritz_mats[which], precision=highest)  51.1 us
    unnamed x1, blocking collectives  39.3 us
    reduce_sum x1, other arithmetic, per_device(): local_terms = jnp.sum(ritz_mats * grad_tile[None], axis=(1, 2))  35.5 us
    dot_general x1, matrix products, per_device(): lax.dot_general(acts_all, lax.all_gather(query_grads, 'row', axis=0, tile...  13.7 us
    all_gather x1, blocking collectives, per_device(): acts_all = lax.all_gather(query_acts, 'col', axis=0, tiled=True)  7.38 us
    all_to_all x1, starting transfers between devices, per_device(): lax.all_to_all(train_acts, 'row', split_axis=1, concat_axis=0, tiled=True)  7.32 us
  transfers between devices with their start and end apart: 3, of which 2 were waited for; matrix products, arithmetic and copies ran while one was open for 17% of the time, Pallas kernels for 0%

profile of v1, /device:TPU:0, one launch (start us, length us, event | category | flops | bytes accessed | tf_op | source)
XLA Modules:
  0.0 302.3 jit_solution(11861154336957036385)
XLA Ops:
  7.2 0.0 all-gather.3.cloned.1.call-start
  7.2 0.7 all-gather.3.cloned.1.call-update
  7.9 7.3 %all-to-all-start = ((bf16[8,8,1024]{2,0,1:T(8,128)(2,1)}), bf16[8,8,1024]{2,0,1:T(8,128)(2,1)S(1)}, u32[]{:S(2)}, u32[]{:S(2)}) async-start(bf16[8,8,1024]{2,0,1:T(8,128)(2,1)} %bitcast.34), calls=%async_computation | async-start | bytes 262144 | tf_op jit(solution)/shard_map/all_to_all | solution.py:33
  15.2 0.0 reduce-scatter.2.cloned.1.call-start
  15.3 7.4 %all_gather.12 = bf16[256,1024]{1,0:T(8,128)(2,1)S(1)} all-gather(bf16[64,1024]{1,0:T(8,128)(2,1)} %param.6), channel_id=1, replica_groups=mesh['row'=8,'col'=4] {'col'}, dimensions={0}, use_global_device_ids=true | all-gather | bytes 655360 | tf_op jit(solution)/shard_map/all_gather | solution.py:23
  22.7 56.5 %all-gather.3.cloned.1.call-done = bf16[256,7168]{1,0:T(8,128)(2,1)} async-done(((bf16[32,7168]{1,0:T(8,128)(2,1)}), bf16[256,7168]{1,0:T(8,128)(2,1)}) %all-gather.3.cloned.1.call-update) | async-done | bytes 3670032 | tf_op jit(solution)/shard_map/all_gather | solution.py:26
  79.1 13.7 %fusion.28 = f32[1024,7168]{1,0:T(8,128)} fusion(bf16[256,1024]{1,0:T(8,128)(2,1)S(1)} %all_gather.12, bf16[256,7168]{1,0:T(8,128)(2,1)} %all-gather.3.cloned.1.call-done), kind=kOutput, calls=%fused_computation.22 | convolution fusion | flops 3758096384 | bytes 33554432 | tf_op jit(solution)/shard_map/dot_general | solution.py:24
  92.8 0.0 copy-start.1
  92.8 35.5 %multiply_reduce_fusion = f32[3]{0:T(128)S(1)} fusion(f32[3,1024,7168]{2,1,0:T(8,128)} %param.8, f32[1024,7168]{1,0:T(8,128)} %fusion.28), kind=kLoop, calls=%fused_computation | loop fusion | flops 44040188 | bytes 117440528 | tf_op jit(solution)/shard_map/reduce_sum | solution.py:30
  128.4 0.2 dynamic-update-slice
  128.6 39.3 %all-reduce = f32[96]{0:T(128)S(1)} all-reduce(f32[96]{0:T(128)S(1)} %dynamic-update-slice), channel_id=2, replica_groups=mesh['row'=8,'col'=4] {'row','col'}, use_global_device_ids=true, to_apply=%add | all-reduce | flops 96 | bytes 768
  167.9 0.1 reshape.8
  168.0 0.0 copy-done.1
  168.0 0.7 fusion.27
  168.7 0.0 all-to-all-done
  168.7 15.6 %fusion.15 = f32[64,7168]{1,0:T(8,128)S(1)} fusion(f32[3,1024,7168]{2,1,0:T(8,128)} %param.8, f32[]{:T(128)} %bitcast.5, bf16[8,8,1024]{2,0,1:T(8,128)(2,1)S(1)} %all-to-all-done), kind=kOutput, calls=%fused_computation.12 | convolution fusion | flops 5637603328 | bytes 31326720 | tf_op jit(solution)/shard_map/dot_general | solution.py:39
  184.3 18.0 %fusion.12 = f32[64,7168]{1,0:T(8,128)S(1)} fusion(f32[64,7168]{1,0:T(8,128)S(1)} %fusion.15, f32[3,1024,7168]{2,1,0:T(8,128)} %param.8, f32[]{:T(128)} %bitcast, bf16[8,8,1024]{2,0,1:T(8,128)(2,1)S(1)} %all-to-all-done), kind=kOutput, calls=%fused_computation.11 | convolution fusion | flops 5638062080 | bytes 33161728 | tf_op jit(solution)/shard_map/dot_general | solution.py:39
  202.3 0.0 copy-start
  202.3 17.5 %fusion.21 = f32[64,7168]{1,0:T(8,128)} fusion(f32[64,7168]{1,0:T(8,128)S(1)} %fusion.12, f32[3,1024,7168]{2,1,0:T(8,128)} %param.8, f32[]{:T(128)} %bitcast.8, bf16[8,8,1024]{2,0,1:T(8,128)(2,1)S(1)} %all-to-all-done), kind=kOutput, calls=%fused_computation.14 | convolution fusion | flops 5638062080 | bytes 33161728 | tf_op jit(solution)/shard_map/dot_general | solution.py:39
  219.8 0.0 reduce-scatter.2.cloned.1.call-update
  219.8 67.6 %reduce-scatter.2.cloned.1.call-done = f32[8,7168]{1,0:T(8,128)} async-done(((f32[64,7168]{1,0:T(8,128)}), f32[8,7168]{1,0:T(8,128)}) %reduce-scatter.2.cloned.1.call-update) | async-done | bytes 229392 | tf_op jit(solution)/shard_map/reduce_scatter | solution.py:40
  287.4 0.0 copy-done
  287.5 1.8 multiply_reduce_fusion.1
  289.3 6.2 %psum.7 = f32[8]{0:T(128)} all-reduce(f32[8]{0:T(128)S(1)} %broadcast_multiply_fusion), channel_id=1, replica_groups=mesh['row'=8,'col'=4] {'col'}, use_global_device_ids=true, to_apply=%region_4.0 | all-reduce | flops 8 | bytes 64 | tf_op jit(solution)/shard_map/psum | solution.py:42
  (4 shorter events, 0.0 us)
Async XLA Ops:
  7.2 72.0 %all-gather.3.cloned.1.call-start = ((), (), s32[]{:S(2)}) async-start(), calls=%async_computation.2 | async-start | bytes 4128768 | tf_op jit(solution)/shard_map/all_gather | solution.py:26
  7.9 160.8 %all-to-all-start = ((bf16[8,8,1024]{2,0,1:T(8,128)(2,1)}), bf16[8,8,1024]{2,0,1:T(8,128)(2,1)S(1)}, u32[]{:S(2)}, u32[]{:S(2)}) async-start(bf16[8,8,1024]{2,0,1:T(8,128)(2,1)} %bitcast.34), calls=%async_computation | async-start | bytes 262144 | tf_op jit(solution)/shard_map/all_to_all | solution.py:33
  15.2 272.2 %reduce-scatter.2.cloned.1.call-start = ((), (), s32[]{:S(2)}) async-start(), calls=%async_computation.3 | async-start | bytes 2064384 | tf_op jit(solution)/shard_map/reduce_scatter | solution.py:40
  92.8 75.2 %copy-start.1 = (f32[3]{0:T(128)S(1)}, f32[3]{0:T(128)}, u32[]{:S(2)}) copy-start(f32[3]{0:T(128)} %param.9) | copy-start | bytes 40
  202.3 85.2 %copy-start = (bf16[8,7168]{1,0:T(8,128)(2,1)S(1)}, bf16[8,7168]{1,0:T(8,128)(2,1)}, u32[]{:S(2)}) copy-start(bf16[8,7168]{1,0:T(8,128)(2,1)} %param.11) | copy-start | bytes 344068
Sparse Core Ops, SparseCore 0:
  10.2 68.9 all-gather.2
  219.9 67.4 reduce-scatter.1

commit v2 on v0

--- a/solution.py
+++ b/solution.py
@@ -3,10 +3,17 @@
 import jax.numpy as jnp
 from jax import lax
 from jax.sharding import PartitionSpec as P
+from jax.lax import psum
 
 D_OUT = 28672
 QUERY = 256
 highest = lax.Precision.HIGHEST
+
+
+def link_sample(local_block, row_axis, a_name):
+    for dev_i in (row_axis, a_name):
+        local_block = psum(local_block, axis_name=dev_i)
+    return local_block
 
 
 def per_device(query_acts, query_grads, ritz_mats, eigenvalues, train_acts, train_grads):
@@ -19,7 +26,7 @@
         preferred_element_type=jnp.float32,
     )
     local_terms = jnp.sum(ritz_mats * grad_tile[None], axis=(1, 2))
-    coeffs = lax.psum(local_terms, ("row", "col"))
+    coeffs = link_sample(local_terms, "col", "row")
     weights = coeffs / (eigenvalues * math.sqrt(QUERY * D_OUT))
     train_local = lax.all_to_all(train_acts, "row", split_axis=1, concat_axis=0, tiled=True).astype(
         jnp.float32

time: 307 us -> 291 us (0.948)
  blocking collectives: 55.7 us -> 42.6 us
    psum x1 -> x2, blocking collectives: 40.7 us -> 27.6 us  [link_sample(): local_block = psum(local_block, axis_name=dev_i)]
    reduce_scatter x1, waiting for transfers between devices: 67.2 us -> 64.1 us  [per_device(): lax.psum_scatter(total, 'row', scatter_dimension=0, tiled=True)]
where the time goes in v2:
time: 291 us
  waiting for transfers between devices  127 us (44%)
  matrix products  64.8 us (22%)
  blocking collectives  42.6 us (15%)
  other arithmetic  37.4 us (13%)
  between operations  14.1 us (5%)
  starting transfers between devices  4.1 us (1%)
    reduce_scatter x1, waiting for transfers between devices, per_device(): lax.psum_scatter(total, 'row', scatter_dimension=0, tiled=True)  64.1 us
    all_gather x1, waiting for transfers between devices, per_device(): lax.all_gather(query_grads, 'row', axis=0, tiled=True)  62.4 us
    dot_general x3, matrix products, per_device(): jnp.dot(train_local, ritz_mats[which], precision=highest)  51.1 us
    reduce_sum x1, other arithmetic, per_device(): local_terms = jnp.sum(ritz_mats * grad_tile[None], axis=(1, 2))  35.5 us
    psum x2, blocking collectives, link_sample(): local_block = psum(local_block, axis_name=dev_i)  27.6 us
    dot_general x1, matrix products, per_device(): lax.dot_general(acts_all, lax.all_gather(query_grads, 'row', axis=0, tile...  13.7 us
    all_gather x1, blocking collectives, per_device(): acts_all = lax.all_gather(query_acts, 'col', axis=0, tiled=True)  8.86 us
    psum x1, blocking collectives, per_device(): scores = lax.psum(score_terms, 'col')  6.17 us
  transfers between devices with their start and end apart: 3, of which 2 were waited for; matrix products, arithmetic and copies ran while one was open for 0% of the time, Pallas kernels for 0%

profile of v2, /device:TPU:0, one launch (start us, length us, event | category | flops | bytes accessed | tf_op | source)
XLA Modules:
  0.0 290.8 jit_solution(17317847330949286920)
XLA Ops:
  7.2 0.0 all-gather.2.cloned.1.call-start
  7.2 0.7 all-gather.2.cloned.1.call-update
  7.9 8.9 %all_gather.6 = bf16[256,1024]{1,0:T(8,128)(2,1)S(1)} all-gather(bf16[64,1024]{1,0:T(8,128)(2,1)} %param.6), channel_id=1, replica_groups=mesh['row'=8,'col'=4] {'col'}, dimensions={0}, use_global_device_ids=true | all-gather | bytes 655360 | tf_op jit(solution)/shard_map/all_gather | solution.py:21
  16.8 62.4 %all-gather.2.cloned.1.call-done = bf16[256,7168]{1,0:T(8,128)(2,1)} async-done(((bf16[32,7168]{1,0:T(8,128)(2,1)}), bf16[256,7168]{1,0:T(8,128)(2,1)}) %all-gather.2.cloned.1.call-update) | async-done | bytes 3670032 | tf_op jit(solution)/shard_map/all_gather | solution.py:24
  79.1 13.7 %fusion.28 = f32[1024,7168]{1,0:T(8,128)} fusion(bf16[256,1024]{1,0:T(8,128)(2,1)S(1)} %all_gather.6, bf16[256,7168]{1,0:T(8,128)(2,1)} %all-gather.2.cloned.1.call-done), kind=kOutput, calls=%fused_computation.22 | convolution fusion | flops 3758096384 | bytes 33554432 | tf_op jit(solution)/shard_map/dot_general | solution.py:22
  92.8 0.0 copy-start.1
  92.8 35.5 %multiply_reduce_fusion = f32[3]{0:T(128)S(1)} fusion(f32[3,1024,7168]{2,1,0:T(8,128)} %param.8, f32[1024,7168]{1,0:T(8,128)} %fusion.28), kind=kLoop, calls=%fused_computation | loop fusion | flops 44040188 | bytes 117440528 | tf_op jit(solution)/shard_map/reduce_sum | solution.py:28
  128.4 5.7 %psum.21 = f32[3]{0:T(128)S(1)} all-reduce(f32[3]{0:T(128)S(1)} %multiply_reduce_fusion), channel_id=1, replica_groups=mesh['row'=8,'col'=4] {'col'}, use_global_device_ids=true, to_apply=%region_1.0 | all-reduce | flops 3 | bytes 24 | tf_op jit(solution)/shard_map/psum | solution.py:15
  134.0 4.0 %all-to-all-start = ((bf16[8,8,1024]{2,0,1:T(8,128)(2,1)}), bf16[8,8,1024]{2,0,1:T(8,128)(2,1)S(1)}, u32[]{:S(2)}, u32[]{:S(2)}) async-start(bf16[8,8,1024]{2,0,1:T(8,128)(2,1)} %bitcast.1), calls=%async_computation | async-start | bytes 262144 | tf_op jit(solution)/shard_map/all_to_all | solution.py:31
  138.1 0.0 reduce-scatter.2.cloned.1.call-start
  138.1 22.0 %psum.22 = f32[3]{0:T(128)S(1)} all-reduce(f32[3]{0:T(128)S(1)} %psum.21), channel_id=1, replica_groups=mesh['row'=8,'col'=4] {'row'}, use_global_device_ids=true, to_apply=%region_2.0 | all-reduce | flops 3 | bytes 24 | tf_op jit(solution)/shard_map/psum | solution.py:15
  160.1 0.0 copy-done.1
  160.1 0.7 fusion.27
  160.7 0.0 all-to-all-done
  160.8 15.6 %fusion.15 = f32[64,7168]{1,0:T(8,128)S(1)} fusion(f32[3,1024,7168]{2,1,0:T(8,128)} %param.8, f32[]{:T(128)} %bitcast.5, bf16[8,8,1024]{2,0,1:T(8,128)(2,1)S(1)} %all-to-all-done), kind=kOutput, calls=%fused_computation.12 | convolution fusion | flops 5637603328 | bytes 31326720 | tf_op jit(solution)/shard_map/dot_general | solution.py:37
  176.4 18.0 %fusion.12 = f32[64,7168]{1,0:T(8,128)S(1)} fusion(f32[64,7168]{1,0:T(8,128)S(1)} %fusion.15, f32[3,1024,7168]{2,1,0:T(8,128)} %param.8, f32[]{:T(128)} %bitcast, bf16[8,8,1024]{2,0,1:T(8,128)(2,1)S(1)} %all-to-all-done), kind=kOutput, calls=%fused_computation.11 | convolution fusion | flops 5638062080 | bytes 33161728 | tf_op jit(solution)/shard_map/dot_general | solution.py:37
  194.3 0.0 copy-start
  194.3 17.5 %fusion.21 = f32[64,7168]{1,0:T(8,128)} fusion(f32[64,7168]{1,0:T(8,128)S(1)} %fusion.12, f32[3,1024,7168]{2,1,0:T(8,128)} %param.8, f32[]{:T(128)} %bitcast.8, bf16[8,8,1024]{2,0,1:T(8,128)(2,1)S(1)} %all-to-all-done), kind=kOutput, calls=%fused_computation.14 | convolution fusion | flops 5638062080 | bytes 33161728 | tf_op jit(solution)/shard_map/dot_general | solution.py:37
  211.8 0.0 reduce-scatter.2.cloned.1.call-update
  211.9 64.1 %reduce-scatter.2.cloned.1.call-done = f32[8,7168]{1,0:T(8,128)} async-done(((f32[64,7168]{1,0:T(8,128)}), f32[8,7168]{1,0:T(8,128)}) %reduce-scatter.2.cloned.1.call-update) | async-done | bytes 229392 | tf_op jit(solution)/shard_map/reduce_scatter | solution.py:38
  275.9 0.0 copy-done
  275.9 1.8 multiply_reduce_fusion.1
  277.8 6.2 %psum.23 = f32[8]{0:T(128)} all-reduce(f32[8]{0:T(128)S(1)} %broadcast_multiply_fusion), channel_id=1, replica_groups=mesh['row'=8,'col'=4] {'col'}, use_global_device_ids=true, to_apply=%region_5.0 | all-reduce | flops 8 | bytes 64 | tf_op jit(solution)/shard_map/psum | solution.py:40
  (2 shorter events, 0.0 us)
Async XLA Ops:
  7.2 72.0 %all-gather.2.cloned.1.call-start = ((), (), s32[]{:S(2)}) async-start(), calls=%async_computation.2 | async-start | bytes 4128768 | tf_op jit(solution)/shard_map/all_gather | solution.py:24
  92.8 67.2 %copy-start.1 = (f32[3]{0:T(128)S(1)}, f32[3]{0:T(128)}, u32[]{:S(2)}) copy-start(f32[3]{0:T(128)} %param.9) | copy-start | bytes 40
  134.0 26.7 %all-to-all-start = ((bf16[8,8,1024]{2,0,1:T(8,128)(2,1)}), bf16[8,8,1024]{2,0,1:T(8,128)(2,1)S(1)}, u32[]{:S(2)}, u32[]{:S(2)}) async-start(bf16[8,8,1024]{2,0,1:T(8,128)(2,1)} %bitcast.1), calls=%async_computation | async-start | bytes 262144 | tf_op jit(solution)/shard_map/all_to_all | solution.py:31
  138.1 137.9 %reduce-scatter.2.cloned.1.call-start = ((), (), s32[]{:S(2)}) async-start(), calls=%async_computation.3 | async-start | bytes 2064384 | tf_op jit(solution)/shard_map/reduce_scatter | solution.py:38
  194.3 81.6 %copy-start = (bf16[8,7168]{1,0:T(8,128)(2,1)S(1)}, bf16[8,7168]{1,0:T(8,128)(2,1)}, u32[]{:S(2)}) copy-start(bf16[8,7168]{1,0:T(8,128)(2,1)} %param.11) | copy-start | bytes 344068
Sparse Core Ops, SparseCore 0:
  10.2 68.9 all-gather.1
  212.0 63.9 reduce-scatter.1
